TPU v7x, 256 devices: a whole 4x4x8 slice. The times are simulated.
256 devices in a mesh: mem: 8 (over z), reg: 32 (over y, x, core).
Axes of the slice: x: 4, y: 4, z: 8, core: 2. Of those that a mesh axis runs over, the one named last changes fastest.
Arguments:
- member_values: float32 [80, 524288], P('mem', 'reg'), may hold values from -6 to 6
- obs_value: float32 [524288], P('reg'), may hold values from -6 to 6
- obs_weight: float32 [524288], P('reg'), may hold values from 0.25 to 4
- obs_cell: int32 [524288], P('reg'), may hold values from -1 to 61439, as said below
Outputs:
- deviation: float32 [80, 61440], P('mem', 'reg')
- departure: float32 [61440], P('reg')
- variance: float32 [61440], P('reg')
- error_variance: float32 [61440], P('reg')
- obs_total: int32 [61440], P('reg')
Inputs may be any that keep to these rules, and one draw needn't show every extreme that they name: `obs_cell`: cell c is owned by region c // 1920. The 16384 slots of one region are 32 blocks of 512 slots, block r holding only cells owned by region r, live slots first and -1 in the empty ones. Every block has at least 128 live slots; one owner's block is full in every region.
All inputs are finite; a program needn't handle non-finite values.
Results may differ from a plain program's by a relative error of at most 0.0003.
Values sent between devices are 32-bit elements; how exact they have to be, the bound alone decides.
A program may use at most 64 MiB of HBM per device.

v0:
```python
import jax
import jax.numpy as jnp
from jax import lax
from jax.sharding import PartitionSpec as P

CELL_DEV = 1920


def sent_to_all(array, axis):
    copies = jnp.broadcast_to(array, (lax.axis_size(axis), *array.shape))
    return lax.all_to_all(copies, axis, split_axis=0, concat_axis=0, tiled=True)


def taken_together(array, axis):
    return sent_to_all(array, axis).sum(axis=0)


def packed_total(arrays, axis):
    line, at, done = (jnp.concatenate([a.reshape(-1) for a in arrays]), 0, [])
    so_far = taken_together(line, axis)
    for a in arrays:
        done.append(so_far[at : at + a.size].reshape(a.shape))
        at += a.size
    return tuple(done)


def shards(member_values, obs_value, obs_weight, obs_cell):
    regions = lax.axis_size("reg")
    groups = lax.axis_size("mem")
    obs_dev = obs_cell.shape[0]
    capacity = obs_dev // regions
    live = obs_cell >= 0
    weight = jnp.where(live, obs_weight, jnp.float32(0.0))
    local_cell = jnp.where(live, obs_cell % CELL_DEV, 0).astype(jnp.float32)
    weighted_members = member_values * weight[None, :]
    meta_rows = jnp.stack([weight * obs_value, weight, local_cell])
    member_buffer = weighted_members.reshape(weighted_members.shape[0], regions, capacity)
    meta_buffer = meta_rows.reshape(3, regions, capacity)
    payload = jnp.concatenate([member_buffer, meta_buffer], 0)
    received = lax.all_to_all(payload, "reg", split_axis=1, concat_axis=1, tiled=True)
    received = received.reshape(received.shape[0], -1)
    members_in = received[:-3]
    meta_in = received[-3:]
    cell_in = meta_in[2].astype(jnp.int32)
    filled_flag = (meta_in[1] > 0).astype(jnp.float32)
    columns = jnp.concatenate([members_in, meta_in[:2], filled_flag[None, :]], 0)
    total_rows = columns.shape[1]
    block_rows = 1024
    column_blocks = columns.reshape(
        columns.shape[0], total_rows // block_rows, block_rows
    ).transpose(1, 0, 2)
    cell_blocks = cell_in.reshape(total_rows // block_rows, block_rows)
    cell_range = jnp.arange(CELL_DEV, dtype=jnp.int32)

    def add_block(carry, inputs):
        block_columns, block_cells = inputs
        one_hot = (block_cells[:, None] == cell_range[None, :]).astype(jnp.float32)
        return (
            carry
            + jnp.dot(
                block_columns,
                one_hot,
                precision=lax.Precision.HIGHEST,
                preferred_element_type=jnp.float32,
            ),
            None,
        )

    start_sums = jnp.zeros((columns.shape[0], CELL_DEV), jnp.float32)
    cell_sums, _ = lax.scan(add_block, start_sums, (column_blocks, cell_blocks))
    counted = cell_sums[-1]
    filled = counted > 0
    weight_total = jnp.where(filled, cell_sums[-2], jnp.float32(1.0))
    superob = cell_sums[:-3] / weight_total[None, :]
    observed_mean = cell_sums[-3] / weight_total
    ensemble = member_values.shape[0] * groups
    moment_one, moment_two = packed_total(
        (jnp.sum(superob, 0), jnp.sum(superob * superob, 0)), "mem"
    )
    ens_mean = moment_one / ensemble
    deviation = superob - ens_mean[None, :]
    variance = (moment_two - moment_one * ens_mean) / (ensemble - 1)
    departure = observed_mean - ens_mean
    error_variance = jnp.where(filled, 1.0 / weight_total, jnp.float32(0.0))
    return (deviation, departure, variance, error_variance, counted.astype(jnp.int32))


def solution(mesh):
    return jax.shard_map(
        shards,
        mesh=mesh,
        in_specs=(P("mem", "reg"), P("reg"), P("reg"), P("reg")),
        out_specs=(P("mem", "reg"), P("reg"), P("reg"), P("reg"), P("reg")),
        check_vma=False,
    )
```

profile of v0, /device:TPU:1, one launch (start us, length us, event | category | flops | bytes accessed | tf_op | source)
XLA Modules:
  0.0 93.8 jit_solution(3885263154804095131)
XLA Ops:
  0.6 0.9 fusion.6
  1.5 0.9 fusion.12
  2.5 1.3 %broadcast_multiply_fusion = f32[10,16384]{1,0:T(8,128)S(1)} fusion(f32[10,16384]{1,0:T(8,128)} %param.6, f32[16384]{0:T(1024)S(1)} %get-tuple-element.84), kind=kLoop, calls=%fused_computation.10 | loop fusion | flops 163840 | bytes 1376256 | tf_op jit(solution)/shard_map/mul | solution.py:35
  3.8 0.6 copy.30
  4.5 0.1 pad_maximum_fusion
  4.6 1.5 %copy.21 = f32[13,32,512]{2,0,1:T(8,128)} copy(f32[13,32,512]{2,1,0:T(8,128)S(1)} %pad_maximum_fusion) | data formatting | bytes 1703936 | tf_op jit(solution)/shard_map/concatenate | solution.py:39
  6.1 8.6 %all-to-all-start = ((f32[13,32,512]{2,0,1:T(8,128)}), f32[13,32,512]{2,0,1:T(8,128)S(1)}, u32[]{:S(2)}, u32[]{:S(2)}) async-start(f32[13,32,512]{2,0,1:T(8,128)} %copy.21), calls=%async_computation | async-start | bytes 2097152 | tf_op jit(solution)/shard_map/all_to_all | solution.py:40
  14.7 17.0 %all-to-all-done = f32[13,32,512]{2,0,1:T(8,128)S(1)} async-done(((f32[13,32,512]{2,0,1:T(8,128)}), f32[13,32,512]{2,0,1:T(8,128)S(1)}, u32[]{:S(2)}, u32[]{:S(2)}) %all-to-all-start) | async-done | bytes 852000 | tf_op jit(solution)/shard_map/all_to_all | solution.py:40
  31.7 0.2 fusion.8
  31.9 0.2 fusion.7
  32.2 0.1 slice.50
  32.3 0.4 copy.22
  32.7 0.2 concatenate.17
  33.0 0.1 maximum_bitcast_fusion
  33.0 42.6 %while.11 = (s32[]{:T(128)}, f32[13,1920]{1,0:T(8,128)S(1)}, f32[16,13,1024]{2,0,1:T(8,128)S(1)}, s32[16,1024]{1,0:T(8,128)S(1)}, s32[]{:T(128)}, /*index=5*/s32[]{:T(128)}) while((s32[]{:T(128)}, f32[13,1920]{1,0:T(8,128)S(1)}, f32[16,13,1024]{2,0,1:T(8,128)S(1)}, s32[16,1024]{1,0:T(8,128)S(1)}, s32[]{:T(128)}, ...), condition=%wide.region_1.2_spmd.clone, body=%wide.region_0.1_spmd.clone.sunk | while | flops 308724480 | bytes 371807 | solution.py:70
  33.1 2.6 %fusion.14 = f32[13,1920]{1,0:T(8,128)S(1)} fusion(s32[1024]{0:T(1024)S(1)} %bitcast.17, f32[13,1920]{1,0:T(8,128)S(1)} %get-tuple-element.121, f32[1,13,1024]{2,0,1:T(1,128)S(1)} %constant_dynamic-slice_fusion.5, pred[]{:T(512)S(6)} %compare.3), kind=kOutput, calls=%fused_computation.4.clone.1 | convolution fusion | flops 308724480 | bytes 257025 | tf_op jit(solution)/shard_map/while/body/eval_jaxpr/dot_general | solution.py:60
  35.8 2.6 %fusion.14 = f32[13,1920]{1,0:T(8,128)S(1)} fusion(s32[1024]{0:T(1024)S(1)} %bitcast.17, f32[13,1920]{1,0:T(8,128)S(1)} %get-tuple-element.121, f32[1,13,1024]{2,0,1:T(1,128)S(1)} %constant_dynamic-slice_fusion.5, pred[]{:T(512)S(6)} %compare.3), kind=kOutput, calls=%fused_computation.4.clone.1 | convolution fusion | flops 308724480 | bytes 257025 | tf_op jit(solution)/shard_map/while/body/eval_jaxpr/dot_general | solution.py:60
  38.5 2.6 %fusion.14 = f32[13,1920]{1,0:T(8,128)S(1)} fusion(s32[1024]{0:T(1024)S(1)} %bitcast.17, f32[13,1920]{1,0:T(8,128)S(1)} %get-tuple-element.121, f32[1,13,1024]{2,0,1:T(1,128)S(1)} %constant_dynamic-slice_fusion.5, pred[]{:T(512)S(6)} %compare.3), kind=kOutput, calls=%fused_computation.4.clone.1 | convolution fusion | flops 308724480 | bytes 257025 | tf_op jit(solution)/shard_map/while/body/eval_jaxpr/dot_general | solution.py:60
  41.1 2.6 %fusion.14 = f32[13,1920]{1,0:T(8,128)S(1)} fusion(s32[1024]{0:T(1024)S(1)} %bitcast.17, f32[13,1920]{1,0:T(8,128)S(1)} %get-tuple-element.121, f32[1,13,1024]{2,0,1:T(1,128)S(1)} %constant_dynamic-slice_fusion.5, pred[]{:T(512)S(6)} %compare.3), kind=kOutput, calls=%fused_computation.4.clone.1 | convolution fusion | flops 308724480 | bytes 257025 | tf_op jit(solution)/shard_map/while/body/eval_jaxpr/dot_general | solution.py:60
  43.8 2.6 %fusion.14 = f32[13,1920]{1,0:T(8,128)S(1)} fusion(s32[1024]{0:T(1024)S(1)} %bitcast.17, f32[13,1920]{1,0:T(8,128)S(1)} %get-tuple-element.121, f32[1,13,1024]{2,0,1:T(1,128)S(1)} %constant_dynamic-slice_fusion.5, pred[]{:T(512)S(6)} %compare.3), kind=kOutput, calls=%fused_computation.4.clone.1 | convolution fusion | flops 308724480 | bytes 257025 | tf_op jit(solution)/shard_map/while/body/eval_jaxpr/dot_general | solution.py:60
  46.4 2.6 %fusion.14 = f32[13,1920]{1,0:T(8,128)S(1)} fusion(s32[1024]{0:T(1024)S(1)} %bitcast.17, f32[13,1920]{1,0:T(8,128)S(1)} %get-tuple-element.121, f32[1,13,1024]{2,0,1:T(1,128)S(1)} %constant_dynamic-slice_fusion.5, pred[]{:T(512)S(6)} %compare.3), kind=kOutput, calls=%fused_computation.4.clone.1 | convolution fusion | flops 308724480 | bytes 257025 | tf_op jit(solution)/shard_map/while/body/eval_jaxpr/dot_general | solution.py:60
  49.1 2.6 %fusion.14 = f32[13,1920]{1,0:T(8,128)S(1)} fusion(s32[1024]{0:T(1024)S(1)} %bitcast.17, f32[13,1920]{1,0:T(8,128)S(1)} %get-tuple-element.121, f32[1,13,1024]{2,0,1:T(1,128)S(1)} %constant_dynamic-slice_fusion.5, pred[]{:T(512)S(6)} %compare.3), kind=kOutput, calls=%fused_computation.4.clone.1 | convolution fusion | flops 308724480 | bytes 257025 | tf_op jit(solution)/shard_map/while/body/eval_jaxpr/dot_general | solution.py:60
  51.8 2.6 %fusion.14 = f32[13,1920]{1,0:T(8,128)S(1)} fusion(s32[1024]{0:T(1024)S(1)} %bitcast.17, f32[13,1920]{1,0:T(8,128)S(1)} %get-tuple-element.121, f32[1,13,1024]{2,0,1:T(1,128)S(1)} %constant_dynamic-slice_fusion.5, pred[]{:T(512)S(6)} %compare.3), kind=kOutput, calls=%fused_computation.4.clone.1 | convolution fusion | flops 308724480 | bytes 257025 | tf_op jit(solution)/shard_map/while/body/eval_jaxpr/dot_general | solution.py:60
  54.4 2.6 %fusion.14 = f32[13,1920]{1,0:T(8,128)S(1)} fusion(s32[1024]{0:T(1024)S(1)} %bitcast.17, f32[13,1920]{1,0:T(8,128)S(1)} %get-tuple-element.121, f32[1,13,1024]{2,0,1:T(1,128)S(1)} %constant_dynamic-slice_fusion.5, pred[]{:T(512)S(6)} %compare.3), kind=kOutput, calls=%fused_computation.4.clone.1 | convolution fusion | flops 308724480 | bytes 257025 | tf_op jit(solution)/shard_map/while/body/eval_jaxpr/dot_general | solution.py:60
  57.1 2.6 %fusion.14 = f32[13,1920]{1,0:T(8,128)S(1)} fusion(s32[1024]{0:T(1024)S(1)} %bitcast.17, f32[13,1920]{1,0:T(8,128)S(1)} %get-tuple-element.121, f32[1,13,1024]{2,0,1:T(1,128)S(1)} %constant_dynamic-slice_fusion.5, pred[]{:T(512)S(6)} %compare.3), kind=kOutput, calls=%fused_computation.4.clone.1 | convolution fusion | flops 308724480 | bytes 257025 | tf_op jit(solution)/shard_map/while/body/eval_jaxpr/dot_general | solution.py:60
  59.8 2.6 %fusion.14 = f32[13,1920]{1,0:T(8,128)S(1)} fusion(s32[1024]{0:T(1024)S(1)} %bitcast.17, f32[13,1920]{1,0:T(8,128)S(1)} %get-tuple-element.121, f32[1,13,1024]{2,0,1:T(1,128)S(1)} %constant_dynamic-slice_fusion.5, pred[]{:T(512)S(6)} %compare.3), kind=kOutput, calls=%fused_computation.4.clone.1 | convolution fusion | flops 308724480 | bytes 257025 | tf_op jit(solution)/shard_map/while/body/eval_jaxpr/dot_general | solution.py:60
  62.4 2.6 %fusion.14 = f32[13,1920]{1,0:T(8,128)S(1)} fusion(s32[1024]{0:T(1024)S(1)} %bitcast.17, f32[13,1920]{1,0:T(8,128)S(1)} %get-tuple-element.121, f32[1,13,1024]{2,0,1:T(1,128)S(1)} %constant_dynamic-slice_fusion.5, pred[]{:T(512)S(6)} %compare.3), kind=kOutput, calls=%fused_computation.4.clone.1 | convolution fusion | flops 308724480 | bytes 257025 | tf_op jit(solution)/shard_map/while/body/eval_jaxpr/dot_general | solution.py:60
  65.1 2.6 %fusion.14 = f32[13,1920]{1,0:T(8,128)S(1)} fusion(s32[1024]{0:T(1024)S(1)} %bitcast.17, f32[13,1920]{1,0:T(8,128)S(1)} %get-tuple-element.121, f32[1,13,1024]{2,0,1:T(1,128)S(1)} %constant_dynamic-slice_fusion.5, pred[]{:T(512)S(6)} %compare.3), kind=kOutput, calls=%fused_computation.4.clone.1 | convolution fusion | flops 308724480 | bytes 257025 | tf_op jit(solution)/shard_map/while/body/eval_jaxpr/dot_general | solution.py:60
  67.8 2.6 %fusion.14 = f32[13,1920]{1,0:T(8,128)S(1)} fusion(s32[1024]{0:T(1024)S(1)} %bitcast.17, f32[13,1920]{1,0:T(8,128)S(1)} %get-tuple-element.121, f32[1,13,1024]{2,0,1:T(1,128)S(1)} %constant_dynamic-slice_fusion.5, pred[]{:T(512)S(6)} %compare.3), kind=kOutput, calls=%fused_computation.4.clone.1 | convolution fusion | flops 308724480 | bytes 257025 | tf_op jit(solution)/shard_map/while/body/eval_jaxpr/dot_general | solution.py:60
  70.4 2.6 %fusion.14 = f32[13,1920]{1,0:T(8,128)S(1)} fusion(s32[1024]{0:T(1024)S(1)} %bitcast.17, f32[13,1920]{1,0:T(8,128)S(1)} %get-tuple-element.121, f32[1,13,1024]{2,0,1:T(1,128)S(1)} %constant_dynamic-slice_fusion.5, pred[]{:T(512)S(6)} %compare.3), kind=kOutput, calls=%fused_computation.4.clone.1 | convolution fusion | flops 308724480 | bytes 257025 | tf_op jit(solution)/shard_map/while/body/eval_jaxpr/dot_general | solution.py:60
  73.1 2.6 %fusion.14 = f32[13,1920]{1,0:T(8,128)S(1)} fusion(s32[1024]{0:T(1024)S(1)} %bitcast.17, f32[13,1920]{1,0:T(8,128)S(1)} %get-tuple-element.121, f32[1,13,1024]{2,0,1:T(1,128)S(1)} %constant_dynamic-slice_fusion.5, pred[]{:T(512)S(6)} %compare.3), kind=kOutput, calls=%fused_computation.4.clone.1 | convolution fusion | flops 308724480 | bytes 257025 | tf_op jit(solution)/shard_map/while/body/eval_jaxpr/dot_general | solution.py:60
  75.7 0.1 slice_reduce_fusion.1
  75.7 0.1 fusion.11
  75.8 0.7 broadcast_in_dim.31
  76.5 8.2 %all-to-all-start.1 = ((f32[8,1,3840]{2,1,0:T(1,128)}), f32[8,1,3840]{2,1,0:T(1,128)S(1)}, u32[]{:S(2)}, u32[]{:S(2)}) async-start(f32[8,1,3840]{2,1,0:T(1,128)} %broadcast_in_dim.31), calls=%async_computation.1 | async-start | bytes 245760 | tf_op jit(solution)/shard_map/all_to_all | solution.py:11
  84.7 0.6 convert_reduce_fusion
  85.4 7.0 %all-to-all-done.1 = f32[8,1,3840]{2,1,0:T(1,128)S(1)} async-done(((f32[8,1,3840]{2,1,0:T(1,128)}), f32[8,1,3840]{2,1,0:T(1,128)S(1)}, u32[]{:S(2)}, u32[]{:S(2)}) %all-to-all-start.1) | async-done | bytes 122912 | tf_op jit(solution)/shard_map/all_to_all | solution.py:11
  92.4 0.1 reduce_sum.29
  92.5 0.6 fusion.9
  93.1 0.7 broadcast_subtract_fusion
  (43 shorter events, 1.2 us)
Async XLA Ops:
  6.1 25.6 %all-to-all-start = ((f32[13,32,512]{2,0,1:T(8,128)}), f32[13,32,512]{2,0,1:T(8,128)S(1)}, u32[]{:S(2)}, u32[]{:S(2)}) async-start(f32[13,32,512]{2,0,1:T(8,128)} %copy.21), calls=%async_computation | async-start | bytes 2097152 | tf_op jit(solution)/shard_map/all_to_all | solution.py:40
  76.5 15.9 %all-to-all-start.1 = ((f32[8,1,3840]{2,1,0:T(1,128)}), f32[8,1,3840]{2,1,0:T(1,128)S(1)}, u32[]{:S(2)}, u32[]{:S(2)}) async-start(f32[8,1,3840]{2,1,0:T(1,128)} %broadcast_in_dim.31), calls=%async_computation.1 | async-start | bytes 245760 | tf_op jit(solution)/shard_map/all_to_all | solution.py:11
where the time goes:
time: 94.2 us; the launch traced here: 93.8 us
  matrix products  41.1 us (44%)
  waiting for transfers between devices  24.1 us (26%)
  starting transfers between devices  16.8 us (18%)
  other arithmetic  5.86 us (6%)
  local copies, waits for them, and re-layouts  4.63 us (5%)
    dot_general x16, matrix products, add_block(): jnp.dot(block_columns, one_hot, precision=lax.Precision.HIGHEST, preferre...  41.1 us
    all_to_all x1, waiting for transfers between devices, shards(): lax.all_to_all(payload, 'reg', split_axis=1, concat_axis=1, tiled=True)  17 us
    all_to_all x1, starting transfers between devices, shards(): lax.all_to_all(payload, 'reg', split_axis=1, concat_axis=1, tiled=True)  8.58 us
    all_to_all x1, starting transfers between devices, sent_to_all(): return lax.all_to_all(copies, axis, split_axis=0, concat_axis=0, tiled=True)  8.19 us
    all_to_all x1, waiting for transfers between devices, sent_to_all(): return lax.all_to_all(copies, axis, split_axis=0, concat_axis=0, tiled=True)  7.02 us
  transfers between devices with their start and end apart: 2, of which 2 were waited for; matrix products, arithmetic and copies ran while one was open for 1% of the time, Pallas kernels for 0%

commit v1 on v0

v1 whole, which is shorter than its diff:
```python
import functools

import jax
import jax.numpy as jnp
from jax import lax
from jax.experimental import pallas as pl
from jax.experimental.pallas import tpu as pltpu
from jax.sharding import PartitionSpec as P

CELL_DEV = 1920
LO = 256
HI = 8
ROWS = 16
PIECES = 3
GROUP = 4
MESH = pl.DeviceIdType.MESH


def kernel(
    regions, zs, members, cap,
    mem_hbm, val_hbm, wgt_hbm, cell_hbm,
    dev_ref, dep_ref, var_ref, err_ref, cnt_ref,
    mem_buf, v_buf, w_buf, c_buf, acc, stat, keep, zbuf,
    send_sem, recv_sem, zsend_sem, zrecv_sem,
):
    lanes = cap // 128
    me = lax.axis_index("reg")
    z = lax.axis_index("mem")
    core, col, row = me % 2, (me // 2) % 4, me // 8

    def peer(k):
        return ((row + k // 8) % 4) * 8 + ((col + (k // 2) % 4) % 4) * 2 + (core + k % 2) % 2

    barrier = pltpu.get_barrier_semaphore()

    def greet(k, _):
        pl.semaphore_signal(barrier, inc=1, device_id={"reg": peer(k)}, device_id_type=MESH)
        return 0

    lax.fori_loop(1, regions, greet, 0)

    def greet_z(j, _):
        pl.semaphore_signal(barrier, inc=1, device_id={"mem": (z + j) % zs}, device_id_type=MESH)
        return 0

    lax.fori_loop(1, zs, greet_z, 0)

    def pieces_of(k, to):
        columns = pl.ds(pl.multiple_of(to * cap, cap), cap)
        return (
            (mem_hbm.at[:, columns], mem_buf.at[k]),
            (val_hbm.at[to], v_buf.at[k]),
            (wgt_hbm.at[to], w_buf.at[k]),
            (cell_hbm.at[to], c_buf.at[k]),
        )

    own = [
        pltpu.make_async_copy(src, dst, recv_sem.at[i, 0])
        for i, (src, dst) in enumerate(pieces_of(0, me))
    ]
    for copy in own:
        copy.start()
    acc[...] = jnp.zeros_like(acc)
    pl.semaphore_wait(barrier, regions + zs - 2)

    def remote(k):
        to = peer(k)
        return [
            pltpu.make_async_remote_copy(
                src_ref=src, dst_ref=dst,
                send_sem=send_sem.at[i, k], recv_sem=recv_sem.at[i, k],
                device_id={"reg": to}, device_id_type=MESH,
            )
            for i, (src, dst) in enumerate(pieces_of(k, to))
        ]

    def send(k, _):
        for copy in remote(k)[::-1]:
            copy.start()
        return 0

    lax.fori_loop(1, regions, send, 0)

    base = me * CELL_DEV
    row_id = lax.broadcasted_iota(jnp.int32, (8, 128), 0)
    iota16 = lax.broadcasted_iota(jnp.int32, (16, 128), 0)
    one = jnp.ones((16, 128), jnp.bfloat16)
    zero = jnp.zeros((16, 128), jnp.bfloat16)
    lo_ids = [(iota16 + 16 * t).astype(jnp.float32).astype(jnp.bfloat16) for t in range(LO // 16)]

    def slot(k):
        left, right = [], []
        for a in range(lanes):
            at = pl.ds(a * 128, 128)
            w = jnp.broadcast_to(w_buf[k, pl.ds(a, 1), :], (8, 128))
            v = jnp.broadcast_to(v_buf[k, pl.ds(a, 1), :], (8, 128))
            c = jnp.broadcast_to(c_buf[k, pl.ds(a, 1), :], (16, 128)) - base
            top = mem_buf[k, pl.ds(0, 8), at] * w
            low = jnp.concatenate([mem_buf[k, pl.ds(8, members - 8), at], jnp.zeros((16 - members, 128), jnp.float32)], 0) * w
            low = jnp.where(row_id == 2, w, jnp.where(row_id == 3, 1.0, jnp.where(row_id == 4, w * v, low)))
            low = jnp.where(row_id < 5, low, 0.0)
            both = jnp.concatenate([top, low], 0)
            parts = []
            for p in range(PIECES):
                part = both.astype(jnp.bfloat16)
                parts.append(part)
                both = both - part.astype(jnp.float32)
            hi = (c >> 8).astype(jnp.float32).astype(jnp.bfloat16)
            lo = (c & 255).astype(jnp.float32).astype(jnp.bfloat16)
            masks = [hi == jnp.bfloat16(h) for h in range(HI)]
            left.append(jnp.concatenate([jnp.where(m, part, zero) for part in parts for m in masks], 0))
            right.append(jnp.concatenate([jnp.where(lo == ids, one, zero) for ids in lo_ids], 0))
        return left, right

    def group(g, _):
        left, right = [], []
        for j in range(GROUP):
            k = g * GROUP + j

            @pl.when(k == 0)
            def _():
                for copy in own:
                    copy.wait()

            @pl.when(k > 0)
            def _():
                for copy in remote(k):
                    copy.wait_recv()

            a, b = slot(k)
            left += a
            right += b
        acc[...] += lax.dot_general(
            jnp.concatenate(left, 1), jnp.concatenate(right, 1),
            (((1,), (1,)), ((), ())), preferred_element_type=jnp.float32,
        )
        return 0

    lax.fori_loop(0, regions // GROUP, group, 0)

    step = HI * ROWS
    sums = acc[pl.ds(0, step), :]
    for p in range(1, PIECES):
        sums = sums + acc[pl.ds(p * step, step), :]
    rows8 = lax.broadcasted_iota(jnp.int32, (8, LO), 0)
    for h in range(HI):
        top = sums[h * ROWS : h * ROWS + 8]
        low = sums[h * ROWS + 8 : h * ROWS + 16]
        weight, count, value = low[2:3], low[3:4], low[4:5]
        total = jnp.where(count > 0, weight, 1.0)
        top = top / total
        low = jnp.where(rows8 < members - 8, low / total, 0.0)
        one_sum = jnp.sum(top + low, 0, keepdims=True)
        mean = one_sum / members
        d_top = top - mean
        d_low = jnp.where(rows8 < members - 8, low - mean, 0.0)
        two = jnp.sum(d_top * d_top + d_low * d_low, 0, keepdims=True)
        for q in range(LO // 128):
            r = h * (LO // 128) + q
            cut = slice(q * 128, q * 128 + 128)
            stat[0, pl.ds(r, 1), :] = one_sum[:, cut]
            stat[1, pl.ds(r, 1), :] = two[:, cut]
            keep[0, pl.ds(r, 1), :] = total[:, cut]
            keep[1, pl.ds(r, 1), :] = count[:, cut]
            keep[2, pl.ds(r, 1), :] = value[:, cut]
            if r * 128 < CELL_DEV:
                dev_ref[pl.ds(0, 8), pl.ds(r * 128, 128)] = top[:, cut]
                dev_ref[pl.ds(8, members - 8), pl.ds(r * 128, 128)] = low[: members - 8, cut]

    def remote_z(j):
        return pltpu.make_async_remote_copy(
            src_ref=stat, dst_ref=zbuf.at[j],
            send_sem=zsend_sem.at[j], recv_sem=zrecv_sem.at[j],
            device_id={"mem": (z + j) % zs}, device_id_type=MESH,
        )

    for j in range(1, zs):
        remote_z(j).start()
    for j in range(1, zs):
        remote_z(j).wait_recv()

    firsts = [stat[0]] + [zbuf[j, 0] for j in range(1, zs)]
    seconds = [stat[1]] + [zbuf[j, 1] for j in range(1, zs)]
    ensemble = members * zs
    mean = functools.reduce(jnp.add, firsts) / ensemble
    spread = functools.reduce(jnp.add, seconds)
    for first in firsts:
        off = first / members - mean
        spread = spread + members * (off * off)
    n_rows = CELL_DEV // 128
    total, count = keep[0], keep[1]
    filled = count > 0
    departure = keep[2] / total - mean
    variance = spread / (ensemble - 1)
    error = jnp.where(filled, 1.0 / total, 0.0)
    dep_ref[...] = departure[:n_rows]
    var_ref[...] = variance[:n_rows]
    err_ref[...] = error[:n_rows]
    cnt_ref[...] = count.astype(jnp.int32)[:n_rows]
    for r in range(n_rows):
        at = pl.ds(r * 128, 128)
        dev_ref[:, at] = dev_ref[:, at] - mean[r : r + 1]

    def drain(k, _):
        for copy in remote(k):
            copy.wait_send()
        return 0

    lax.fori_loop(1, regions, drain, 0)
    for j in range(1, zs):
        remote_z(j).wait_send()


def shards(member_values, obs_value, obs_weight, obs_cell):
    regions = lax.axis_size("reg")
    zs = lax.axis_size("mem")
    members, obs = member_values.shape
    cap = obs // regions
    blocks = (regions, cap // 128, 128)
    n_rows = CELL_DEV // 128
    flat = jax.ShapeDtypeStruct((n_rows, 128), jnp.float32)
    any_spec = pl.BlockSpec(memory_space=pl.ANY)
    vmem = pl.BlockSpec(memory_space=pltpu.VMEM)
    dev, dep, var, err, cnt = pl.pallas_call(
        functools.partial(kernel, regions, zs, members, cap),
        out_shape=(
            jax.ShapeDtypeStruct((members, CELL_DEV), jnp.float32),
            flat, flat, flat,
            jax.ShapeDtypeStruct((n_rows, 128), jnp.int32),
        ),
        in_specs=[any_spec] * 4,
        out_specs=(vmem,) * 5,
        scratch_shapes=[
            pltpu.VMEM((regions, members, cap), jnp.float32),
            pltpu.VMEM(blocks, jnp.float32),
            pltpu.VMEM(blocks, jnp.float32),
            pltpu.VMEM(blocks, jnp.int32),
            pltpu.VMEM((PIECES * HI * ROWS, LO), jnp.float32),
            pltpu.VMEM((2, 16, 128), jnp.float32),
            pltpu.VMEM((3, 16, 128), jnp.float32),
            pltpu.VMEM((zs, 2, 16, 128), jnp.float32),
            pltpu.SemaphoreType.DMA((4, regions)),
            pltpu.SemaphoreType.DMA((4, regions)),
            pltpu.SemaphoreType.DMA((zs,)),
            pltpu.SemaphoreType.DMA((zs,)),
        ],
        compiler_params=pltpu.CompilerParams(collective_id=0, has_side_effects=True),
        name="superob",
    )(
        member_values,
        obs_value.reshape(blocks),
        obs_weight.reshape(blocks),
        obs_cell.reshape(blocks),
    )
    return dev, dep.reshape(-1), var.reshape(-1), err.reshape(-1), cnt.reshape(-1)


def solution(mesh):
    return jax.shard_map(
        shards,
        mesh=mesh,
        in_specs=(P("mem", "reg"), P("reg"), P("reg"), P("reg")),
        out_specs=(P("mem", "reg"), P("reg"), P("reg"), P("reg"), P("reg")),
        check_vma=False,
    )
```

time: 94.2 us -> 46.5 us (0.49)
  Pallas kernels: 0 us -> 41.4 us
  matrix products: 41.1 us -> 0 us
  waiting for transfers between devices: 24.1 us -> 0 us
  starting transfers between devices: 16.8 us -> 0 us
  other arithmetic: 5.86 us -> 0 us
    pallas_call x0 -> x1, Pallas kernels: none -> 41.4 us  [shards(): pl.pallas_call(functools.partial(kernel, regions, zs, members, cap), out_...]
    dot_general x16 -> x0, matrix products: 41.1 us -> none  [add_block(): jnp.dot(block_columns, one_hot, precision=lax.Precision.HIGHEST, preferre...]
    all_to_all x2 -> x0, waiting for transfers between devices: 24.1 us -> none  [the longest x1 17 us: shards(): lax.all_to_all(payload, 'reg', split_axis=1, concat_axis=1, tiled=True)]
    all_to_all x2 -> x0, starting transfers between devices: 16.8 us -> none  [the longest x1 8.58 us: shards(): lax.all_to_all(payload, 'reg', split_axis=1, concat_axis=1, tiled=True)]
    unnamed x1 -> x13, local copies, waits for them, and re-layouts: 0.61 us -> 4.27 us
    mul x2 -> x0, other arithmetic: 2.23 us -> none  [the longest x1 1.31 us: shards(): weighted_members = member_values * weight[None, :]]
    convert_element_type x4 -> x0, other arithmetic: 1.93 us -> none  [the longest x1 0.89 us: shards(): local_cell = jnp.where(live, obs_cell % CELL_DEV, 0).astype(jnp.float32)]
    concatenate x3 -> x0, local copies, waits for them, and re-layouts: 1.75 us -> none  [the longest x1 1.5 us: shards(): payload = jnp.concatenate([member_buffer, meta_buffer], 0)]
  transfers between devices with their start and end apart: 2 -> 0, of which waited for: 2 -> 0; matrix products, arithmetic and copies ran while one was open for 1% -> 0% of each run, Pallas kernels for 0% -> 0%
where the time goes in v1:
time: 46.5 us; the launch traced here: 46.3 us
  Pallas kernels  41.4 us (89%)
  local copies, waits for them, and re-layouts  4.27 us (9%)
  between operations  0.65 us (1%)
    pallas_call x1, Pallas kernels, shards(): pl.pallas_call(functools.partial(kernel, regions, zs, members, cap), out_...  41.4 us
    unnamed x13, local copies, waits for them, and re-layouts  4.27 us

profile of v1, /device:TPU:1, one launch (start us, length us, event | category | flops | bytes accessed | tf_op | source)
XLA Modules:
  0.0 46.3 jit_solution(7584304395421078624)
XLA Ops:
  0.6 41.4 %superob.1 = (f32[10,1920]{1,0:T(8,128)}, f32[15,128]{1,0:T(8,128)}, f32[15,128]{1,0:T(8,128)}, f32[15,128]{1,0:T(8,128)}, s32[15,128]{1,0:T(8,128)}) custom-call(f32[10,16384]{1,0:T(8,128)} %mem_hbm.1, f32[32,4,128]{2,1,0:T(4,128)} %bitcast.7, f32[32,4,128]{2,1,0:T(4,128)} %bitcast.8, s32[32,4,128]{2,1,0:T(4,128)} %bitcast.9), custom_call_target="tpu_custom_call" | custom-call | tf_op jit(solution)/shard_map/superob/pallas_call | solution.py:224
  42.0 0.0 copy-start.3
  42.0 1.6 %copy.14 = f32[10,1920]{1,0:T(8,128)} copy(f32[10,1920]{1,0:T(8,128)} %get-tuple-element.20) | data formatting | bytes 153600
  43.6 0.0 copy-done.3
  43.6 0.0 copy-start.2
  43.6 0.6 %copy.15 = f32[1920]{0:T(1024)} copy(f32[1920]{0:T(1024)S(1)} %bitcast.13) | data formatting | bytes 15360
  44.2 0.1 copy-done.2
  44.3 0.0 copy-start.1
  44.3 0.6 %copy.16 = f32[1920]{0:T(1024)} copy(f32[1920]{0:T(1024)S(1)} %bitcast.12) | data formatting | bytes 15360
  44.9 0.1 copy-done.1
  45.0 0.0 copy-start
  45.0 0.6 %copy.17 = f32[1920]{0:T(1024)} copy(f32[1920]{0:T(1024)S(1)} %bitcast.11) | data formatting | bytes 15360
  45.6 0.1 copy-done
  45.7 0.6 %copy.18 = s32[1920]{0:T(1024)} copy(s32[1920]{0:T(1024)S(1)} %bitcast.10) | data formatting | bytes 15360
Async XLA Ops:
  42.0 1.6 %copy-start.3 = (f32[15,128]{1,0:T(8,128)S(1)}, f32[15,128]{1,0:T(8,128)}, u32[]{:S(2)}) copy-start(f32[15,128]{1,0:T(8,128)} %get-tuple-element.11) | copy-start | bytes 23044
  43.6 0.7 %copy-start.2 = (f32[15,128]{1,0:T(8,128)S(1)}, f32[15,128]{1,0:T(8,128)}, u32[]{:S(2)}) copy-start(f32[15,128]{1,0:T(8,128)} %get-tuple-element.12) | copy-start | bytes 23044
  44.3 0.7 %copy-start.1 = (f32[15,128]{1,0:T(8,128)S(1)}, f32[15,128]{1,0:T(8,128)}, u32[]{:S(2)}) copy-start(f32[15,128]{1,0:T(8,128)} %get-tuple-element.13) | copy-start | bytes 23044
  45.0 0.7 %copy-start = (s32[15,128]{1,0:T(8,128)S(1)}, s32[15,128]{1,0:T(8,128)}, u32[]{:S(2)}) copy-start(s32[15,128]{1,0:T(8,128)} %get-tuple-element.14) | copy-start | bytes 23044

commit v2 on v1

--- a/solution.py
+++ b/solution.py
@@ -20,8 +20,8 @@
     regions, zs, members, cap,
     mem_hbm, val_hbm, wgt_hbm, cell_hbm,
     dev_ref, dep_ref, var_ref, err_ref, cnt_ref,
-    mem_buf, v_buf, w_buf, c_buf, acc, stat, keep, zbuf,
-    send_sem, recv_sem, zsend_sem, zrecv_sem,
+    mem_buf, ext_src, ext_buf, c_buf, acc, stat, keep, zbuf,
+    stage_sem, send_sem, recv_sem, zsend_sem, zrecv_sem,
 ):
     lanes = cap // 128
     me = lax.axis_index("reg")
@@ -48,19 +48,45 @@
     def pieces_of(k, to):
         columns = pl.ds(pl.multiple_of(to * cap, cap), cap)
         return (
-            (mem_hbm.at[:, columns], mem_buf.at[k]),
-            (val_hbm.at[to], v_buf.at[k]),
-            (wgt_hbm.at[to], w_buf.at[k]),
+            (mem_hbm.at[pl.ds(0, 8), columns], mem_buf.at[k]),
+            (ext_src.at[to], ext_buf.at[k]),
             (cell_hbm.at[to], c_buf.at[k]),
         )
 
+    def stage(r):
+        columns = pl.ds(pl.multiple_of(r * cap, cap), cap)
+        return pltpu.make_async_copy(
+            mem_hbm.at[pl.ds(8, members - 8), columns],
+            ext_src.at[r, pl.ds(0, members - 8)],
+            stage_sem.at[r],
+        )
+
+    extra = [
+        pltpu.make_async_copy(src, ext_src.at[:, pl.ds(at, 1), :], stage_sem.at[regions + i])
+        for i, (src, at) in enumerate(((wgt_hbm, members - 8), (val_hbm, members - 7)))
+    ]
+    for copy in extra:
+        copy.start()
+
+    def start_stage(r, _):
+        stage(r).start()
+        return 0
+
+    def wait_stage(r, _):
+        stage(r).wait()
+        return 0
+
+    lax.fori_loop(0, regions, start_stage, 0)
+    acc[...] = jnp.zeros_like(acc)
+    lax.fori_loop(0, regions, wait_stage, 0)
+    for copy in extra:
+        copy.wait()
     own = [
         pltpu.make_async_copy(src, dst, recv_sem.at[i, 0])
         for i, (src, dst) in enumerate(pieces_of(0, me))
     ]
     for copy in own:
         copy.start()
-    acc[...] = jnp.zeros_like(acc)
     pl.semaphore_wait(barrier, regions + zs - 2)
 
     def remote(k):
@@ -92,11 +118,11 @@
         left, right = [], []
         for a in range(lanes):
             at = pl.ds(a * 128, 128)
-            w = jnp.broadcast_to(w_buf[k, pl.ds(a, 1), :], (8, 128))
-            v = jnp.broadcast_to(v_buf[k, pl.ds(a, 1), :], (8, 128))
+            w = jnp.broadcast_to(ext_buf[k, pl.ds(members - 8, 1), at], (8, 128))
+            v = jnp.broadcast_to(ext_buf[k, pl.ds(members - 7, 1), at], (8, 128))
             c = jnp.broadcast_to(c_buf[k, pl.ds(a, 1), :], (16, 128)) - base
             top = mem_buf[k, pl.ds(0, 8), at] * w
-            low = jnp.concatenate([mem_buf[k, pl.ds(8, members - 8), at], jnp.zeros((16 - members, 128), jnp.float32)], 0) * w
+            low = jnp.concatenate([ext_buf[k, pl.ds(0, members - 8), at], jnp.zeros((16 - members, 128), jnp.float32)], 0) * w
             low = jnp.where(row_id == 2, w, jnp.where(row_id == 3, 1.0, jnp.where(row_id == 4, w * v, low)))
             low = jnp.where(row_id < 5, low, 0.0)
             both = jnp.concatenate([top, low], 0)
@@ -211,6 +237,11 @@
         remote_z(j).wait_send()
 
 
+def settle(dev_in, dep_in, var_in, err_in, cnt_in, dev, dep, var, err, cnt):
+    for src, dst in ((dev_in, dev), (dep_in, dep), (var_in, var), (err_in, err), (cnt_in, cnt)):
+        dst[...] = src[...]
+
+
 def shards(member_values, obs_value, obs_weight, obs_cell):
     regions = lax.axis_size("reg")
     zs = lax.axis_size("mem")
@@ -221,37 +252,48 @@
     flat = jax.ShapeDtypeStruct((n_rows, 128), jnp.float32)
     any_spec = pl.BlockSpec(memory_space=pl.ANY)
     vmem = pl.BlockSpec(memory_space=pltpu.VMEM)
-    dev, dep, var, err, cnt = pl.pallas_call(
+    shapes = (
+        jax.ShapeDtypeStruct((members, CELL_DEV), jnp.float32),
+        flat, flat, flat,
+        jax.ShapeDtypeStruct((n_rows, 128), jnp.int32),
+    )
+    results = pl.pallas_call(
         functools.partial(kernel, regions, zs, members, cap),
-        out_shape=(
-            jax.ShapeDtypeStruct((members, CELL_DEV), jnp.float32),
-            flat, flat, flat,
-            jax.ShapeDtypeStruct((n_rows, 128), jnp.int32),
-        ),
+        out_shape=shapes,
         in_specs=[any_spec] * 4,
         out_specs=(vmem,) * 5,
         scratch_shapes=[
-            pltpu.VMEM((regions, members, cap), jnp.float32),
-            pltpu.VMEM(blocks, jnp.float32),
-            pltpu.VMEM(blocks, jnp.float32),
+            pltpu.VMEM((regions, 8, cap), jnp.float32),
+            pltpu.VMEM((regions, members - 6, cap), jnp.float32),
+            pltpu.VMEM((regions, members - 6, cap), jnp.float32),
             pltpu.VMEM(blocks, jnp.int32),
             pltpu.VMEM((PIECES * HI * ROWS, LO), jnp.float32),
             pltpu.VMEM((2, 16, 128), jnp.float32),
             pltpu.VMEM((3, 16, 128), jnp.float32),
             pltpu.VMEM((zs, 2, 16, 128), jnp.float32),
-            pltpu.SemaphoreType.DMA((4, regions)),
-            pltpu.SemaphoreType.DMA((4, regions)),
+            pltpu.SemaphoreType.DMA((regions + 2,)),
+            pltpu.SemaphoreType.DMA((3, regions)),
+            pltpu.SemaphoreType.DMA((3, regions)),
             pltpu.SemaphoreType.DMA((zs,)),
             pltpu.SemaphoreType.DMA((zs,)),
         ],
-        compiler_params=pltpu.CompilerParams(collective_id=0, has_side_effects=True),
+        compiler_params=pltpu.CompilerParams(collective_id=0, has_side_effects=True, vmem_limit_bytes=8 << 20),
         name="superob",
     )(
-        member_values,
-        obs_value.reshape(blocks),
-        obs_weight.reshape(blocks),
-        obs_cell.reshape(blocks),
+        *(
+            pltpu.with_memory_space_constraint(a, pltpu.HBM)
+            for a in (
+                member_values,
+                obs_value.reshape(regions, 1, cap),
+                obs_weight.reshape(regions, 1, cap),
+                obs_cell.reshape(blocks),
+            )
+        )
     )
+    dev, dep, var, err, cnt = pl.pallas_call(
+        settle, out_shape=shapes, in_specs=[vmem] * 5, out_specs=(vmem,) * 5, name="settle",
+        compiler_params=pltpu.CompilerParams(vmem_limit_bytes=1 << 20),
+    )(*results)
     return dev, dep.reshape(-1), var.reshape(-1), err.reshape(-1), cnt.reshape(-1)
 
 

time: 46.5 us -> 36.3 us (0.78)
  Pallas kernels: 41.4 us -> 35.5 us
  local copies, waits for them, and re-layouts: 4.27 us -> 0 us
    pallas_call x1, Pallas kernels: 41.4 us -> 34.8 us  [shards(): pl.pallas_call(functools.partial(kernel, regions, zs, members, cap), out_...]
    unnamed x13 -> x0, local copies, waits for them, and re-layouts: 4.27 us -> none
    pallas_call x0 -> x1, Pallas kernels: none -> 0.67 us  [shards(): pl.pallas_call(settle, out_shape=shapes, in_specs=[vmem] * 5, out_specs=(...]
where the time goes in v2:
time: 36.3 us; the launch traced here: 36.1 us
  Pallas kernels  35.5 us (98%)
  between operations  0.64 us (2%)
    pallas_call x1, Pallas kernels, shards(): pl.pallas_call(functools.partial(kernel, regions, zs, members, cap), out_...  34.8 us

profile of v2, /device:TPU:1, one launch (start us, length us, event | category | flops | bytes accessed | tf_op | source)
XLA Modules:
  0.0 36.1 jit_solution(17427984158460930569)
XLA Ops:
  0.6 34.8 %superob.1 = (f32[10,1920]{1,0:T(8,128)S(1)}, f32[15,128]{1,0:T(8,128)S(1)}, f32[15,128]{1,0:T(8,128)S(1)}, f32[15,128]{1,0:T(8,128)S(1)}, s32[15,128]{1,0:T(8,128)S(1)}) custom-call(f32[10,16384]{1,0:T(8,128)} %mem_hbm.1, f32[32,1,512]{2,1,0:T(1,128)} %bitcast.7, f32[32,1,512]{2,1,0:T(1,128)} %bitcast.8, s32[32,4,128]{2,1,0:T(4,128)} %bitcast.9), custom_call_target="tpu_custom_call" | custom-call | tf_op jit(solution)/shard_map/superob/pallas_call | solution.py:260
  35.4 0.7 %settle.1 = (f32[10,1920]{1,0:T(8,128)}, f32[15,128]{1,0:T(8,128)}, f32[15,128]{1,0:T(8,128)}, f32[15,128]{1,0:T(8,128)}, s32[15,128]{1,0:T(8,128)}) custom-call(f32[10,1920]{1,0:T(8,128)S(1)} %get-tuple-element.15.dev_in, f32[15,128]{1,0:T(8,128)S(1)} %get-tuple-element.16.dep_in, f32[15,128]{1,0:T(8,128)S(1)} %get-tuple-element.17.var_in, ...), custom_call_target="tpu_custom_call" | custom-call | tf_op jit(solution)/shard_map/settle/pallas_call | solution.py:293

commit v3 on v2

--- a/solution.py
+++ b/solution.py
@@ -14,6 +14,17 @@
 PIECES = 3
 GROUP = 4
 MESH = pl.DeviceIdType.MESH
+
+
+def hops(shift):
+    return sum(min(d, 4 - d) for d in shift[:2])
+
+
+SHIFTS = sorted(
+    ((dy, dx, dc) for dc in range(2) for dy in range(4) for dx in range(4) if dy or dx or dc),
+    key=hops,
+)
+GROUPS = (4,) * 8
 
 
 def kernel(
@@ -28,22 +39,17 @@
     z = lax.axis_index("mem")
     core, col, row = me % 2, (me // 2) % 4, me // 8
 
-    def peer(k):
-        return ((row + k // 8) % 4) * 8 + ((col + (k // 2) % 4) % 4) * 2 + (core + k % 2) % 2
+    def peer(shift):
+        dy, dx, dc = shift
+        return ((row + dy) % 4) * 8 + ((col + dx) % 4) * 2 + (core + dc) % 2
 
     barrier = pltpu.get_barrier_semaphore()
 
-    def greet(k, _):
-        pl.semaphore_signal(barrier, inc=1, device_id={"reg": peer(k)}, device_id_type=MESH)
-        return 0
-
-    lax.fori_loop(1, regions, greet, 0)
-
-    def greet_z(j, _):
+    for j in sorted(range(1, zs), key=lambda j: -min(j, zs - j)):
         pl.semaphore_signal(barrier, inc=1, device_id={"mem": (z + j) % zs}, device_id_type=MESH)
-        return 0
-
-    lax.fori_loop(1, zs, greet_z, 0)
+    peers = [peer(shift) for shift in SHIFTS]
+    for to in peers:
+        pl.semaphore_signal(barrier, inc=1, device_id={"reg": to}, device_id_type=MESH)
 
     def pieces_of(k, to):
         columns = pl.ds(pl.multiple_of(to * cap, cap), cap)
@@ -89,8 +95,7 @@
         copy.start()
     pl.semaphore_wait(barrier, regions + zs - 2)
 
-    def remote(k):
-        to = peer(k)
+    def remote(k, to):
         return [
             pltpu.make_async_remote_copy(
                 src_ref=src, dst_ref=dst,
@@ -100,12 +105,9 @@
             for i, (src, dst) in enumerate(pieces_of(k, to))
         ]
 
-    def send(k, _):
-        for copy in remote(k)[::-1]:
+    for k, to in enumerate(peers):
+        for copy in remote(k + 1, to)[::-1]:
             copy.start()
-        return 0
-
-    lax.fori_loop(1, regions, send, 0)
 
     base = me * CELL_DEV
     row_id = lax.broadcasted_iota(jnp.int32, (8, 128), 0)
@@ -138,21 +140,13 @@
             right.append(jnp.concatenate([jnp.where(lo == ids, one, zero) for ids in lo_ids], 0))
         return left, right
 
-    def group(g, _):
+    def arrived(k):
+        for copy in remote(k, peers[-1]):
+            copy.wait_recv()
+
+    def add(slots):
         left, right = [], []
-        for j in range(GROUP):
-            k = g * GROUP + j
-
-            @pl.when(k == 0)
-            def _():
-                for copy in own:
-                    copy.wait()
-
-            @pl.when(k > 0)
-            def _():
-                for copy in remote(k):
-                    copy.wait_recv()
-
+        for k in slots:
             a, b = slot(k)
             left += a
             right += b
@@ -160,9 +154,28 @@
             jnp.concatenate(left, 1), jnp.concatenate(right, 1),
             (((1,), (1,)), ((), ())), preferred_element_type=jnp.float32,
         )
+
+    for copy in own:
+        copy.wait()
+    for k in range(1, GROUPS[0]):
+        arrived(k)
+    add(range(GROUPS[0]))
+    same = sum(1 for size in GROUPS if size == GROUP)
+
+    def group(g, _):
+        slots = [g * GROUP + j for j in range(GROUP)]
+        for k in slots:
+            arrived(k)
+        add(slots)
         return 0
 
-    lax.fori_loop(0, regions // GROUP, group, 0)
+    lax.fori_loop(1, same, group, 0)
+    at = same * GROUP
+    for size in GROUPS[same:]:
+        for k in range(at, at + size):
+            arrived(k)
+        add(range(at, at + size))
+        at += size
 
     step = HI * ROWS
     sums = acc[pl.ds(0, step), :]
@@ -202,6 +215,9 @@
 
     for j in range(1, zs):
         remote_z(j).start()
+    for k, to in enumerate(peers):
+        for copy in remote(k + 1, to):
+            copy.wait_send()
     for j in range(1, zs):
         remote_z(j).wait_recv()
 
@@ -227,12 +243,6 @@
         at = pl.ds(r * 128, 128)
         dev_ref[:, at] = dev_ref[:, at] - mean[r : r + 1]
 
-    def drain(k, _):
-        for copy in remote(k):
-            copy.wait_send()
-        return 0
-
-    lax.fori_loop(1, regions, drain, 0)
     for j in range(1, zs):
         remote_z(j).wait_send()
 

time: 36.3 us -> 32.2 us (0.89)
  Pallas kernels: 35.5 us -> 31.2 us
    pallas_call x1, Pallas kernels: 34.8 us -> 30.5 us  [shards(): pl.pallas_call(functools.partial(kernel, regions, zs, members, cap), out_...]
where the time goes in v3:
time: 32.2 us; the launch traced here: 31.9 us
  Pallas kernels  31.2 us (97%)
  between operations  0.64 us (2%)
    pallas_call x1, Pallas kernels, shards(): pl.pallas_call(functools.partial(kernel, regions, zs, members, cap), out_...  30.5 us
    pallas_call x1, Pallas kernels, shards(): pl.pallas_call(settle, out_shape=shapes, in_specs=[vmem] * 5, out_specs=(...  0.67 us

profile of v3, /device:TPU:1, one launch (start us, length us, event | category | flops | bytes accessed | tf_op | source)
XLA Modules:
  0.0 31.9 jit_solution(2579557192988800615)
XLA Ops:
  0.6 30.5 %superob.1 = (f32[10,1920]{1,0:T(8,128)S(1)}, f32[15,128]{1,0:T(8,128)S(1)}, f32[15,128]{1,0:T(8,128)S(1)}, f32[15,128]{1,0:T(8,128)S(1)}, s32[15,128]{1,0:T(8,128)S(1)}) custom-call(f32[10,16384]{1,0:T(8,128)} %mem_hbm.1, f32[32,1,512]{2,1,0:T(1,128)} %bitcast.7, f32[32,1,512]{2,1,0:T(1,128)} %bitcast.8, s32[32,4,128]{2,1,0:T(4,128)} %bitcast.9), custom_call_target="tpu_custom_call" | custom-call | tf_op jit(solution)/shard_map/superob/pallas_call | solution.py:270
  31.2 0.7 %settle.1 = (f32[10,1920]{1,0:T(8,128)}, f32[15,128]{1,0:T(8,128)}, f32[15,128]{1,0:T(8,128)}, f32[15,128]{1,0:T(8,128)}, s32[15,128]{1,0:T(8,128)}) custom-call(f32[10,1920]{1,0:T(8,128)S(1)} %get-tuple-element.15.dev_in, f32[15,128]{1,0:T(8,128)S(1)} %get-tuple-element.16.dep_in, f32[15,128]{1,0:T(8,128)S(1)} %get-tuple-element.17.var_in, ...), custom_call_target="tpu_custom_call" | custom-call | tf_op jit(solution)/shard_map/settle/pallas_call | solution.py:303

commit v4 on v3

--- a/solution.py
+++ b/solution.py
@@ -30,9 +30,9 @@
 def kernel(
     regions, zs, members, cap,
     mem_hbm, val_hbm, wgt_hbm, cell_hbm,
-    dev_ref, dep_ref, var_ref, err_ref, cnt_ref,
-    mem_buf, ext_src, ext_buf, c_buf, acc, stat, keep, zbuf,
-    stage_sem, send_sem, recv_sem, zsend_sem, zrecv_sem,
+    dev_ref, mean_ref, dep_ref, var_ref, err_ref, cnt_ref,
+    mem_buf, mem_src, ext_src, ext_buf, v_buf, c_src, acc, stat, keep, obs, zbuf,
+    stage_sem, send_sem, recv_sem, zsend_sem, zrecv_sem, osend_sem, orecv_sem, zreply,
 ):
     lanes = cap // 128
     me = lax.axis_index("reg")
@@ -45,18 +45,22 @@
 
     barrier = pltpu.get_barrier_semaphore()
 
-    for j in sorted(range(1, zs), key=lambda j: -min(j, zs - j)):
-        pl.semaphore_signal(barrier, inc=1, device_id={"mem": (z + j) % zs}, device_id_type=MESH)
     peers = [peer(shift) for shift in SHIFTS]
-    for to in peers:
+    for to in peers[::-1]:
         pl.semaphore_signal(barrier, inc=1, device_id={"reg": to}, device_id_type=MESH)
+    zpeers = [(z + j) % zs for j in range(1, zs)]
+    zahead = [z < other for other in zpeers]
+    for to, early in zip(zpeers, zahead):
+        @pl.when(early)
+        def _():
+            pl.semaphore_signal(barrier, inc=1, device_id={"mem": to}, device_id_type=MESH)
 
     def pieces_of(k, to):
         columns = pl.ds(pl.multiple_of(to * cap, cap), cap)
         return (
-            (mem_hbm.at[pl.ds(0, 8), columns], mem_buf.at[k]),
+            (mem_src.at[:, columns], mem_buf.at[k]),
             (ext_src.at[to], ext_buf.at[k]),
-            (cell_hbm.at[to], c_buf.at[k]),
+            (val_hbm.at[to], v_buf.at[k]),
         )
 
     def stage(r):
@@ -67,9 +71,14 @@
             stage_sem.at[r],
         )
 
+    cell_copy = pltpu.make_async_copy(cell_hbm, c_src, stage_sem.at[regions + 1])
+    cell_copy.start()
+    main_copy = pltpu.make_async_copy(mem_hbm.at[pl.ds(0, 8), :], mem_src, stage_sem.at[regions + 2])
+    main_copy.start()
     extra = [
-        pltpu.make_async_copy(src, ext_src.at[:, pl.ds(at, 1), :], stage_sem.at[regions + i])
-        for i, (src, at) in enumerate(((wgt_hbm, members - 8), (val_hbm, members - 7)))
+        pltpu.make_async_copy(
+            wgt_hbm, ext_src.at[:, pl.ds(members - 8, 1), :], stage_sem.at[regions]
+        )
     ]
     for copy in extra:
         copy.start()
@@ -84,7 +93,15 @@
 
     lax.fori_loop(0, regions, start_stage, 0)
     acc[...] = jnp.zeros_like(acc)
+    cell_copy.wait()
+
+    def place_cell(r, _):
+        ext_src[r, pl.ds(members - 7, 1), :] = c_src[r].astype(jnp.float32)
+        return 0
+
+    lax.fori_loop(0, regions, place_cell, 0, unroll=8)
     lax.fori_loop(0, regions, wait_stage, 0)
+    main_copy.wait()
     for copy in extra:
         copy.wait()
     own = [
@@ -93,21 +110,36 @@
     ]
     for copy in own:
         copy.start()
-    pl.semaphore_wait(barrier, regions + zs - 2)
-
-    def remote(k, to):
+    pl.semaphore_wait(barrier, regions - 1 + z)
+
+    first = z == 0
+
+    def remote(k, to, which):
+        pieces = pieces_of(k, to)
         return [
             pltpu.make_async_remote_copy(
                 src_ref=src, dst_ref=dst,
                 send_sem=send_sem.at[i, k], recv_sem=recv_sem.at[i, k],
                 device_id={"reg": to}, device_id_type=MESH,
             )
-            for i, (src, dst) in enumerate(pieces_of(k, to))
+            for i in which
+            for src, dst in [pieces[i]]
         ]
 
+    @pl.when(first)
+    def _():
+        for k, to in enumerate(peers):
+            remote(k + 1, to, (2,))[0].start()
+
     for k, to in enumerate(peers):
-        for copy in remote(k + 1, to)[::-1]:
-            copy.start()
+        main, ext = remote(k + 1, to, (0, 1))
+        ext.start()
+        main.start()
+
+    for j, (to, early) in enumerate(zip(zpeers, zahead)):
+        @pl.when(jnp.logical_not(early))
+        def _():
+            pl.semaphore_signal(zreply.at[zs - 2 - j], inc=1, device_id={"mem": to}, device_id_type=MESH)
 
     base = me * CELL_DEV
     row_id = lax.broadcasted_iota(jnp.int32, (8, 128), 0)
@@ -121,11 +153,11 @@
         for a in range(lanes):
             at = pl.ds(a * 128, 128)
             w = jnp.broadcast_to(ext_buf[k, pl.ds(members - 8, 1), at], (8, 128))
-            v = jnp.broadcast_to(ext_buf[k, pl.ds(members - 7, 1), at], (8, 128))
-            c = jnp.broadcast_to(c_buf[k, pl.ds(a, 1), :], (16, 128)) - base
+            v = jnp.broadcast_to(v_buf[k, :, at], (8, 128))
+            c = jnp.broadcast_to(ext_buf[k, pl.ds(members - 7, 1), at].astype(jnp.int32), (16, 128)) - base
             top = mem_buf[k, pl.ds(0, 8), at] * w
             low = jnp.concatenate([ext_buf[k, pl.ds(0, members - 8), at], jnp.zeros((16 - members, 128), jnp.float32)], 0) * w
-            low = jnp.where(row_id == 2, w, jnp.where(row_id == 3, 1.0, jnp.where(row_id == 4, w * v, low)))
+            low = jnp.where(row_id == 2, w, jnp.where(row_id == 3, 1.0, jnp.where((row_id == 4) & first, w * v, low)))
             low = jnp.where(row_id < 5, low, 0.0)
             both = jnp.concatenate([top, low], 0)
             parts = []
@@ -141,8 +173,13 @@
         return left, right
 
     def arrived(k):
-        for copy in remote(k, peers[-1]):
-            copy.wait_recv()
+        main, ext = remote(k, peers[-1], (0, 1))
+        ext.wait_recv()
+        main.wait_recv()
+
+        @pl.when(first)
+        def _():
+            remote(k, peers[-1], (2,))[0].wait_recv()
 
     def add(slots):
         left, right = [], []
@@ -201,7 +238,11 @@
             stat[1, pl.ds(r, 1), :] = two[:, cut]
             keep[0, pl.ds(r, 1), :] = total[:, cut]
             keep[1, pl.ds(r, 1), :] = count[:, cut]
-            keep[2, pl.ds(r, 1), :] = value[:, cut]
+
+            @pl.when(first)
+            def _():
+                obs[pl.ds(r, 1), :] = value[:, cut]
+
             if r * 128 < CELL_DEV:
                 dev_ref[pl.ds(0, 8), pl.ds(r * 128, 128)] = top[:, cut]
                 dev_ref[pl.ds(8, members - 8), pl.ds(r * 128, 128)] = low[: members - 8, cut]
@@ -213,11 +254,41 @@
             device_id={"mem": (z + j) % zs}, device_id_type=MESH,
         )
 
-    for j in range(1, zs):
+    def remote_obs(j):
+        return pltpu.make_async_remote_copy(
+            src_ref=obs, dst_ref=obs,
+            send_sem=osend_sem.at[j], recv_sem=orecv_sem.at[0],
+            device_id={"mem": (z + j) % zs}, device_id_type=MESH,
+        )
+
+    for j in range(zs - 1):
+        @pl.when(zahead[j])
+        def _():
+            pl.semaphore_wait(zreply.at[j], 1)
+
+    for j in sorted(range(1, zs), key=lambda j: -min(j, zs - j)):
         remote_z(j).start()
+
+    @pl.when(first)
+    def _():
+        for j in range(1, zs):
+            remote_obs(j).start()
+
     for k, to in enumerate(peers):
-        for copy in remote(k + 1, to):
+        for copy in remote(k + 1, to, (0, 1)):
             copy.wait_send()
+
+    @pl.when(first)
+    def _():
+        for k, to in enumerate(peers):
+            remote(k + 1, to, (2,))[0].wait_send()
+        for j in range(1, zs):
+            remote_obs(j).wait_send()
+
+    @pl.when(jnp.logical_not(first))
+    def _():
+        remote_obs(1).wait_recv()
+
     for j in range(1, zs):
         remote_z(j).wait_recv()
 
@@ -232,24 +303,25 @@
     n_rows = CELL_DEV // 128
     total, count = keep[0], keep[1]
     filled = count > 0
-    departure = keep[2] / total - mean
+    departure = obs[...] / total - mean
     variance = spread / (ensemble - 1)
     error = jnp.where(filled, 1.0 / total, 0.0)
     dep_ref[...] = departure[:n_rows]
     var_ref[...] = variance[:n_rows]
     err_ref[...] = error[:n_rows]
     cnt_ref[...] = count.astype(jnp.int32)[:n_rows]
-    for r in range(n_rows):
-        at = pl.ds(r * 128, 128)
-        dev_ref[:, at] = dev_ref[:, at] - mean[r : r + 1]
+    mean_ref[...] = mean[:n_rows]
 
     for j in range(1, zs):
         remote_z(j).wait_send()
 
 
-def settle(dev_in, dep_in, var_in, err_in, cnt_in, dev, dep, var, err, cnt):
-    for src, dst in ((dev_in, dev), (dep_in, dep), (var_in, var), (err_in, err), (cnt_in, cnt)):
+def settle(sup_in, mean_in, dep_in, var_in, err_in, cnt_in, dev, dep, var, err, cnt):
+    for src, dst in ((dep_in, dep), (var_in, var), (err_in, err), (cnt_in, cnt)):
         dst[...] = src[...]
+    for r in range(CELL_DEV // 128):
+        at = pl.ds(r * 128, 128)
+        dev[:, at] = sup_in[:, at] - mean_in[pl.ds(r, 1), :]
 
 
 def shards(member_values, obs_value, obs_weight, obs_cell):
@@ -257,7 +329,6 @@
     zs = lax.axis_size("mem")
     members, obs = member_values.shape
     cap = obs // regions
-    blocks = (regions, cap // 128, 128)
     n_rows = CELL_DEV // 128
     flat = jax.ShapeDtypeStruct((n_rows, 128), jnp.float32)
     any_spec = pl.BlockSpec(memory_space=pl.ANY)
@@ -269,23 +340,29 @@
     )
     results = pl.pallas_call(
         functools.partial(kernel, regions, zs, members, cap),
-        out_shape=shapes,
+        out_shape=(shapes[0], flat, *shapes[1:]),
         in_specs=[any_spec] * 4,
-        out_specs=(vmem,) * 5,
+        out_specs=(vmem,) * 6,
         scratch_shapes=[
             pltpu.VMEM((regions, 8, cap), jnp.float32),
+            pltpu.VMEM((8, regions * cap), jnp.float32),
             pltpu.VMEM((regions, members - 6, cap), jnp.float32),
             pltpu.VMEM((regions, members - 6, cap), jnp.float32),
-            pltpu.VMEM(blocks, jnp.int32),
+            pltpu.VMEM((regions, 1, cap), jnp.float32),
+            pltpu.VMEM((regions, 1, cap), jnp.int32),
             pltpu.VMEM((PIECES * HI * ROWS, LO), jnp.float32),
             pltpu.VMEM((2, 16, 128), jnp.float32),
-            pltpu.VMEM((3, 16, 128), jnp.float32),
+            pltpu.VMEM((2, 16, 128), jnp.float32),
+            pltpu.VMEM((16, 128), jnp.float32),
             pltpu.VMEM((zs, 2, 16, 128), jnp.float32),
-            pltpu.SemaphoreType.DMA((regions + 2,)),
+            pltpu.SemaphoreType.DMA((regions + 3,)),
             pltpu.SemaphoreType.DMA((3, regions)),
             pltpu.SemaphoreType.DMA((3, regions)),
             pltpu.SemaphoreType.DMA((zs,)),
             pltpu.SemaphoreType.DMA((zs,)),
+            pltpu.SemaphoreType.DMA((zs,)),
+            pltpu.SemaphoreType.DMA((1,)),
+            pltpu.SemaphoreType.REGULAR((zs - 1,)),
         ],
         compiler_params=pltpu.CompilerParams(collective_id=0, has_side_effects=True, vmem_limit_bytes=8 << 20),
         name="superob",
@@ -296,12 +373,12 @@
                 member_values,
                 obs_value.reshape(regions, 1, cap),
                 obs_weight.reshape(regions, 1, cap),
-                obs_cell.reshape(blocks),
+                obs_cell.reshape(regions, 1, cap),
             )
         )
     )
     dev, dep, var, err, cnt = pl.pallas_call(
-        settle, out_shape=shapes, in_specs=[vmem] * 5, out_specs=(vmem,) * 5, name="settle",
+        settle, out_shape=shapes, in_specs=[vmem] * 6, out_specs=(vmem,) * 5, name="settle",
         compiler_params=pltpu.CompilerParams(vmem_limit_bytes=1 << 20),
     )(*results)
     return dev, dep.reshape(-1), var.reshape(-1), err.reshape(-1), cnt.reshape(-1)

time: 32.2 us -> 30.6 us (0.950)
  Pallas kernels: 31.2 us -> 29.9 us
    pallas_call x1, Pallas kernels: 30.5 us -> 29.2 us  [shards(): pl.pallas_call(functools.partial(kernel, regions, zs, members, cap), out_...]
where the time goes in v4:
time: 30.6 us; the launch traced here: 30.5 us
  Pallas kernels  29.9 us (98%)
  between operations  0.64 us (2%)
    pallas_call x1, Pallas kernels, shards(): pl.pallas_call(functools.partial(kernel, regions, zs, members, cap), out_...  29.2 us
    pallas_call x1, Pallas kernels, shards(): pl.pallas_call(settle, out_shape=shapes, in_specs=[vmem] * 6, out_specs=(...  0.68 us

profile of v4, /device:TPU:1, one launch (start us, length us, event | category | flops | bytes accessed | tf_op | source)
XLA Modules:
  0.0 30.5 jit_solution(17594837209152541962)
XLA Ops:
  0.6 29.2 %superob.1 = (f32[10,1920]{1,0:T(8,128)S(1)}, f32[15,128]{1,0:T(8,128)S(1)}, f32[15,128]{1,0:T(8,128)S(1)}, f32[15,128]{1,0:T(8,128)S(1)}, f32[15,128]{1,0:T(8,128)S(1)}, /*index=5*/s32[15,128]{1,0:T(8,128)S(1)}) custom-call(f32[10,16384]{1,0:T(8,128)} %mem_hbm.1, f32[32,1,512]{2,1,0:T(1,128)} %bitcast.7, f32[32,1,512]{2,1,0:T(1,128)} %bitcast.8, ...), custom_call_target="tpu_custom_call" | custom-call | tf_op jit(solution)/shard_map/superob/pallas_call | solution.py:341
  29.8 0.7 %settle.1 = (f32[10,1920]{1,0:T(8,128)}, f32[15,128]{1,0:T(8,128)}, f32[15,128]{1,0:T(8,128)}, f32[15,128]{1,0:T(8,128)}, s32[15,128]{1,0:T(8,128)}) custom-call(f32[10,1920]{1,0:T(8,128)S(1)} %get-tuple-element.16.sup_in, f32[15,128]{1,0:T(8,128)S(1)} %get-tuple-element.17.mean_in, f32[15,128]{1,0:T(8,128)S(1)} %get-tuple-element.18.dep_in, ...), custom_call_target="tpu_custom_call" | custom-call | tf_op jit(solution)/shard_map/settle/pallas_call | solution.py:380

commit v5 on v4

--- a/solution.py
+++ b/solution.py
@@ -24,7 +24,6 @@
     ((dy, dx, dc) for dc in range(2) for dy in range(4) for dx in range(4) if dy or dx or dc),
     key=hops,
 )
-GROUPS = (4,) * 8
 
 
 def kernel(
@@ -46,6 +45,28 @@
     barrier = pltpu.get_barrier_semaphore()
 
     peers = [peer(shift) for shift in SHIFTS]
+    def pieces_of(k, to):
+        columns = pl.ds(pl.multiple_of(to * cap, cap), cap)
+        return (
+            (mem_src.at[:, columns], mem_buf.at[k]),
+            (ext_src.at[:, columns], ext_buf.at[k]),
+            (val_hbm.at[to], v_buf.at[k]),
+        )
+
+    spare = members - 8
+    staged = [
+        pltpu.make_async_copy(src, dst, stage_sem.at[i])
+        for i, (src, dst) in enumerate(
+            (
+                (cell_hbm, c_src),
+                (mem_hbm.at[pl.ds(0, 8), :], mem_src),
+                (mem_hbm.at[pl.ds(8, spare), :], ext_src.at[pl.ds(0, spare), :]),
+                (wgt_hbm, ext_src.at[pl.ds(spare, 1), :]),
+            )
+        )
+    ]
+    for copy in staged:
+        copy.start()
     for to in peers[::-1]:
         pl.semaphore_signal(barrier, inc=1, device_id={"reg": to}, device_id_type=MESH)
     zpeers = [(z + j) % zs for j in range(1, zs)]
@@ -55,54 +76,10 @@
         def _():
             pl.semaphore_signal(barrier, inc=1, device_id={"mem": to}, device_id_type=MESH)
 
-    def pieces_of(k, to):
-        columns = pl.ds(pl.multiple_of(to * cap, cap), cap)
-        return (
-            (mem_src.at[:, columns], mem_buf.at[k]),
-            (ext_src.at[to], ext_buf.at[k]),
-            (val_hbm.at[to], v_buf.at[k]),
-        )
-
-    def stage(r):
-        columns = pl.ds(pl.multiple_of(r * cap, cap), cap)
-        return pltpu.make_async_copy(
-            mem_hbm.at[pl.ds(8, members - 8), columns],
-            ext_src.at[r, pl.ds(0, members - 8)],
-            stage_sem.at[r],
-        )
-
-    cell_copy = pltpu.make_async_copy(cell_hbm, c_src, stage_sem.at[regions + 1])
-    cell_copy.start()
-    main_copy = pltpu.make_async_copy(mem_hbm.at[pl.ds(0, 8), :], mem_src, stage_sem.at[regions + 2])
-    main_copy.start()
-    extra = [
-        pltpu.make_async_copy(
-            wgt_hbm, ext_src.at[:, pl.ds(members - 8, 1), :], stage_sem.at[regions]
-        )
-    ]
-    for copy in extra:
-        copy.start()
-
-    def start_stage(r, _):
-        stage(r).start()
-        return 0
-
-    def wait_stage(r, _):
-        stage(r).wait()
-        return 0
-
-    lax.fori_loop(0, regions, start_stage, 0)
     acc[...] = jnp.zeros_like(acc)
-    cell_copy.wait()
-
-    def place_cell(r, _):
-        ext_src[r, pl.ds(members - 7, 1), :] = c_src[r].astype(jnp.float32)
-        return 0
-
-    lax.fori_loop(0, regions, place_cell, 0, unroll=8)
-    lax.fori_loop(0, regions, wait_stage, 0)
-    main_copy.wait()
-    for copy in extra:
+    staged[0].wait()
+    ext_src[pl.ds(spare + 1, 1), :] = c_src[...].astype(jnp.float32)
+    for copy in staged[1:]:
         copy.wait()
     own = [
         pltpu.make_async_copy(src, dst, recv_sem.at[i, 0])
@@ -194,34 +171,34 @@
 
     for copy in own:
         copy.wait()
-    for k in range(1, GROUPS[0]):
-        arrived(k)
-    add(range(GROUPS[0]))
-    same = sum(1 for size in GROUPS if size == GROUP)
 
     def group(g, _):
         slots = [g * GROUP + j for j in range(GROUP)]
-        for k in slots:
-            arrived(k)
+
+        @pl.when(g == 0)
+        def _():
+            for k in range(1, GROUP):
+                arrived(k)
+
+        @pl.when(g > 0)
+        def _():
+            for k in slots:
+                arrived(k)
+
         add(slots)
         return 0
 
-    lax.fori_loop(1, same, group, 0)
-    at = same * GROUP
-    for size in GROUPS[same:]:
-        for k in range(at, at + size):
-            arrived(k)
-        add(range(at, at + size))
-        at += size
+    lax.fori_loop(0, regions // GROUP, group, 0)
 
     step = HI * ROWS
-    sums = acc[pl.ds(0, step), :]
-    for p in range(1, PIECES):
-        sums = sums + acc[pl.ds(p * step, step), :]
     rows8 = lax.broadcasted_iota(jnp.int32, (8, LO), 0)
-    for h in range(HI):
-        top = sums[h * ROWS : h * ROWS + 8]
-        low = sums[h * ROWS + 8 : h * ROWS + 16]
+
+    def band(h, _):
+        def rows(off):
+            at = pl.multiple_of(h * ROWS + off, 8)
+            return sum(acc[pl.ds(p * step + at, 8), :] for p in range(PIECES))
+
+        top, low = rows(0), rows(8)
         weight, count, value = low[2:3], low[3:4], low[4:5]
         total = jnp.where(count > 0, weight, 1.0)
         top = top / total
@@ -231,6 +208,9 @@
         d_top = top - mean
         d_low = jnp.where(rows8 < members - 8, low - mean, 0.0)
         two = jnp.sum(d_top * d_top + d_low * d_low, 0, keepdims=True)
+        cells = pl.ds(pl.multiple_of(h * LO, LO), LO)
+        dev_ref[pl.ds(0, 8), cells] = top
+        dev_ref[pl.ds(8, members - 8), cells] = low[: members - 8]
         for q in range(LO // 128):
             r = h * (LO // 128) + q
             cut = slice(q * 128, q * 128 + 128)
@@ -243,9 +223,9 @@
             def _():
                 obs[pl.ds(r, 1), :] = value[:, cut]
 
-            if r * 128 < CELL_DEV:
-                dev_ref[pl.ds(0, 8), pl.ds(r * 128, 128)] = top[:, cut]
-                dev_ref[pl.ds(8, members - 8), pl.ds(r * 128, 128)] = low[: members - 8, cut]
+        return 0
+
+    lax.fori_loop(0, HI, band, 0)
 
     def remote_z(j):
         return pltpu.make_async_remote_copy(
@@ -340,22 +320,24 @@
     )
     results = pl.pallas_call(
         functools.partial(kernel, regions, zs, members, cap),
-        out_shape=(shapes[0], flat, *shapes[1:]),
+        out_shape=(
+            jax.ShapeDtypeStruct((members, HI * LO), jnp.float32), flat, *shapes[1:]
+        ),
         in_specs=[any_spec] * 4,
         out_specs=(vmem,) * 6,
         scratch_shapes=[
             pltpu.VMEM((regions, 8, cap), jnp.float32),
             pltpu.VMEM((8, regions * cap), jnp.float32),
-            pltpu.VMEM((regions, members - 6, cap), jnp.float32),
+            pltpu.VMEM((members - 6, regions * cap), jnp.float32),
             pltpu.VMEM((regions, members - 6, cap), jnp.float32),
             pltpu.VMEM((regions, 1, cap), jnp.float32),
-            pltpu.VMEM((regions, 1, cap), jnp.int32),
+            pltpu.VMEM((1, regions * cap), jnp.int32),
             pltpu.VMEM((PIECES * HI * ROWS, LO), jnp.float32),
             pltpu.VMEM((2, 16, 128), jnp.float32),
             pltpu.VMEM((2, 16, 128), jnp.float32),
             pltpu.VMEM((16, 128), jnp.float32),
             pltpu.VMEM((zs, 2, 16, 128), jnp.float32),
-            pltpu.SemaphoreType.DMA((regions + 3,)),
+            pltpu.SemaphoreType.DMA((4,)),
             pltpu.SemaphoreType.DMA((3, regions)),
             pltpu.SemaphoreType.DMA((3, regions)),
             pltpu.SemaphoreType.DMA((zs,)),
@@ -372,8 +354,8 @@
             for a in (
                 member_values,
                 obs_value.reshape(regions, 1, cap),
-                obs_weight.reshape(regions, 1, cap),
-                obs_cell.reshape(regions, 1, cap),
+                obs_weight.reshape(1, -1),
+                obs_cell.reshape(1, -1),
             )
         )
     )

time: 30.6 us -> 30.4 us (level)
  no operation moved by 1% of the time
where the time goes in v5:
time: 30.4 us; the launch traced here: 30.3 us
  Pallas kernels  29.7 us (98%)
  between operations  0.64 us (2%)
    pallas_call x1, Pallas kernels, shards(): pl.pallas_call(functools.partial(kernel, regions, zs, members, cap), out_...  29 us
    pallas_call x1, Pallas kernels, shards(): pl.pallas_call(settle, out_shape=shapes, in_specs=[vmem] * 6, out_specs=(...  0.68 us

profile of v5, /device:TPU:1, one launch (start us, length us, event | category | flops | bytes accessed | tf_op | source)
XLA Modules:
  0.0 30.3 jit_solution(565317616921416960)
XLA Ops:
  0.6 29.0 %superob.1 = (f32[10,2048]{1,0:T(8,128)S(1)}, f32[15,128]{1,0:T(8,128)S(1)}, f32[15,128]{1,0:T(8,128)S(1)}, f32[15,128]{1,0:T(8,128)S(1)}, f32[15,128]{1,0:T(8,128)S(1)}, /*index=5*/s32[15,128]{1,0:T(8,128)S(1)}) custom-call(f32[10,16384]{1,0:T(8,128)} %mem_hbm.1, f32[32,1,512]{2,1,0:T(1,128)} %bitcast.7, f32[1,16384]{1,0:T(1,128)} %bitcast.8, ...), custom_call_target="tpu_custom_call" | custom-call | tf_op jit(solution)/shard_map/superob/pallas_call | solution.py:321
  29.7 0.7 %settle.1 = (f32[10,1920]{1,0:T(8,128)}, f32[15,128]{1,0:T(8,128)}, f32[15,128]{1,0:T(8,128)}, f32[15,128]{1,0:T(8,128)}, s32[15,128]{1,0:T(8,128)}) custom-call(f32[10,2048]{1,0:T(8,128)S(1)} %get-tuple-element.16.sup_in, f32[15,128]{1,0:T(8,128)S(1)} %get-tuple-element.17.mean_in, f32[15,128]{1,0:T(8,128)S(1)} %get-tuple-element.18.dep_in, ...), custom_call_target="tpu_custom_call" | custom-call | tf_op jit(solution)/shard_map/settle/pallas_call | solution.py:362

commit v6 on v5

--- a/solution.py
+++ b/solution.py
@@ -22,7 +22,7 @@
 
 SHIFTS = sorted(
     ((dy, dx, dc) for dc in range(2) for dy in range(4) for dx in range(4) if dy or dx or dc),
-    key=hops,
+    key=lambda shift: (0, 1, 2, 4, 3).index(hops(shift)),
 )
 
 

time: 30.4 us -> 30.2 us (level)
    pallas_call x1, Pallas kernels: 29 us -> 28.7 us  [shards(): pl.pallas_call(functools.partial(kernel, regions, zs, members, cap), out_...]
where the time goes in v6:
time: 30.2 us; the launch traced here: 30 us
  Pallas kernels  29.4 us (97%)
  between operations  0.64 us (2%)
    pallas_call x1, Pallas kernels, shards(): pl.pallas_call(functools.partial(kernel, regions, zs, members, cap), out_...  28.7 us
    pallas_call x1, Pallas kernels, shards(): pl.pallas_call(settle, out_shape=shapes, in_specs=[vmem] * 6, out_specs=(...  0.68 us

profile of v6, /device:TPU:1, one launch (start us, length us, event | category | flops | bytes accessed | tf_op | source)
XLA Modules:
  0.0 30.0 jit_solution(7863520479036492845)
XLA Ops:
  0.6 28.7 %superob.1 = (f32[10,2048]{1,0:T(8,128)S(1)}, f32[15,128]{1,0:T(8,128)S(1)}, f32[15,128]{1,0:T(8,128)S(1)}, f32[15,128]{1,0:T(8,128)S(1)}, f32[15,128]{1,0:T(8,128)S(1)}, /*index=5*/s32[15,128]{1,0:T(8,128)S(1)}) custom-call(f32[10,16384]{1,0:T(8,128)} %mem_hbm.1, f32[32,1,512]{2,1,0:T(1,128)} %bitcast.7, f32[1,16384]{1,0:T(1,128)} %bitcast.8, ...), custom_call_target="tpu_custom_call" | custom-call | tf_op jit(solution)/shard_map/superob/pallas_call | solution.py:321
  29.3 0.7 %settle.1 = (f32[10,1920]{1,0:T(8,128)}, f32[15,128]{1,0:T(8,128)}, f32[15,128]{1,0:T(8,128)}, f32[15,128]{1,0:T(8,128)}, s32[15,128]{1,0:T(8,128)}) custom-call(f32[10,2048]{1,0:T(8,128)S(1)} %get-tuple-element.16.sup_in, f32[15,128]{1,0:T(8,128)S(1)} %get-tuple-element.17.mean_in, f32[15,128]{1,0:T(8,128)S(1)} %get-tuple-element.18.dep_in, ...), custom_call_target="tpu_custom_call" | custom-call | tf_op jit(solution)/shard_map/settle/pallas_call | solution.py:362
